TPU v7x, 256 devices: a whole 4x4x8 slice. The times are simulated.
256 devices in a mesh: seq: 128 (over y, z, x_lo, core), slide: 2 (over x_hi).
Axes of the slice: x: 4 (x_hi: 2, x_lo: 2; x = x_hi * 2 + x_lo), y: 4, z: 8, core: 2. Of those that a mesh axis runs over, the one named last changes fastest.
Arguments:
- layer_input: bfloat16 [2, 32768, 768], P('slide', 'seq'), may hold values from -6 to 6
- cotangent: bfloat16 [2, 32768, 768], P('slide', 'seq'), may hold values from -6 to 6
- layer_norm_gain: float32 [768], replicated, may hold values from 0.25 to 1.75
- layer_norm_bias: float32 [768], replicated, may hold values from -3 to 3
- query_key_value_weight: bfloat16 [768, 2304], replicated, may hold values from -4 to 4
- output_weight: bfloat16 [768, 768], replicated, may hold values from -0.21875 to 0.21875
Outputs:
- layer_output: bfloat16 [2, 32768, 768], P('slide', 'seq')
- input_grad: bfloat16 [2, 32768, 768], P('slide', 'seq')
- grad_qkv: float32 [768, 2304], P('seq')
- grad_out: float32 [768, 768], P('seq')
- grad_gain: float32 [768], replicated
- grad_bias: float32 [768], replicated
All inputs are finite; a program needn't handle non-finite values.
Results may differ from a plain program's by a relative error of at most 0.011.
Values may be sent and summed in bfloat16 or wider, within the bound.
No kernel may reach another device: no remote copies, remote signals or barrier semaphores. Data moves between devices by JAX's collectives and lax.ppermute only.
A program may use at most 128 MiB of HBM per device.

v0:
```python
import jax
import jax.numpy as jnp
from jax import lax
from jax.sharding import Mesh
from jax.sharding import PartitionSpec as P

HEADS = 12
SEQ = ("seq_0", "seq_1", "seq_2", "seq_3")
SEQ_SLIDE = ("seq_0", "seq_1", "seq_2", "seq_3", "slide")
EPS = 1e-05


def from_behind(block, axis, distance):
    devices = range(lax.axis_size(axis))
    route = [(i - distance, i) for i in devices if i - distance in devices]
    return lax.ppermute(block, axis, route)


def one_axis_at_a_time(shard, axes):
    for axis in axes:
        shard = lax.psum(shard, axis)
    return shard


def cut_along(shard, dim, peers):
    before, after = (shard.shape[:dim], shard.shape[dim + 1 :])
    return jnp.moveaxis(shard.reshape(*before, peers, -1, *after), dim, 0)


def sent_and_summed(shard, axis, dim):
    peers = lax.axis_size(axis)
    pieces = lax.all_to_all(cut_along(shard, dim, peers), axis, 0, 0, tiled=True)
    return jnp.sum(pieces.astype(jnp.float32), axis=0)


def summed_rows(shard, axes, dim):
    far, near = axes
    own = sent_and_summed(cut_along(shard, dim, lax.axis_size(far)), near, dim + 1)
    return jnp.sum(
        lax.all_to_all(own.astype(jnp.bfloat16), far, 0, 0, tiled=True).astype(jnp.float32), axis=0
    )


def sent_to_all(shard, axis):
    copies = jnp.broadcast_to(shard, (lax.axis_size(axis), *shard.shape))
    return lax.all_to_all(copies, axis, split_axis=0, concat_axis=0, tiled=True)


def over_copies(shard, axis):
    return sent_to_all(shard, axis).astype(jnp.float32).sum(axis=0)


def apply_layer_norm(token_rows, scale_gain, shift_bias):
    values = token_rows.astype(jnp.float32)
    centered_rows = values - jnp.mean(values, axis=-1, keepdims=True)
    inverse_deviation = lax.rsqrt(
        jnp.mean(centered_rows * centered_rows, axis=-1, keepdims=True) + EPS
    )
    normalized_rows = centered_rows * inverse_deviation
    return (
        (normalized_rows * scale_gain + shift_bias).astype(jnp.bfloat16),
        normalized_rows,
        inverse_deviation,
    )


def attend(qkv_self, memory_key_value, memory_present):
    token_length = qkv_self.shape[0]
    feature_width = memory_key_value.shape[1] // 2
    head_dim = feature_width // HEADS
    query = qkv_self[:, :feature_width].reshape(token_length, HEADS, head_dim)
    keys = jnp.concatenate(
        [memory_key_value[:, :feature_width], qkv_self[:, feature_width : 2 * feature_width]], 0
    ).reshape(2 * token_length, HEADS, head_dim)
    values = jnp.concatenate(
        [memory_key_value[:, feature_width:], qkv_self[:, 2 * feature_width :]], 0
    ).reshape(2 * token_length, HEADS, head_dim)
    scores = jnp.einsum(
        "qhe,khe->hqk", query, keys, preferred_element_type=jnp.float32
    ) * head_dim ** (-0.5)
    row_ids = lax.broadcasted_iota(jnp.int32, (token_length, 2 * token_length), 0)
    col_ids = lax.broadcasted_iota(jnp.int32, (token_length, 2 * token_length), 1)
    allowed = jnp.where(col_ids < token_length, memory_present, col_ids - token_length <= row_ids)
    scores = jnp.where(allowed[None], scores, -1e30)
    top = jnp.max(scores, axis=-1, keepdims=True)
    weights = jnp.exp(scores - top)
    probs = weights / jnp.sum(weights, axis=-1, keepdims=True)
    probs_b = probs.astype(jnp.bfloat16)
    mixed = jnp.einsum("hqk,khe->qhe", probs_b, values, preferred_element_type=jnp.float32)
    mixed = mixed.reshape(token_length, feature_width).astype(jnp.bfloat16)
    return (mixed, probs, probs_b, query, keys, values)


def attend_back(d_mixed, probs, probs_b, query, keys, values):
    token_length, heads, head_dim = query.shape
    grad_heads = d_mixed.reshape(token_length, heads, head_dim)
    d_probs = jnp.einsum("qhe,khe->hqk", grad_heads, values, preferred_element_type=jnp.float32)
    d_scores = probs * (d_probs - jnp.sum(d_probs * probs, axis=-1, keepdims=True))
    d_scores_b = (d_scores * head_dim ** (-0.5)).astype(jnp.bfloat16)
    d_query = jnp.einsum("hqk,khe->qhe", d_scores_b, keys, preferred_element_type=jnp.float32)
    d_keys = jnp.einsum("hqk,qhe->khe", d_scores_b, query, preferred_element_type=jnp.float32)
    d_values = jnp.einsum("hqk,qhe->khe", probs_b, grad_heads, preferred_element_type=jnp.float32)
    return (
        d_query.reshape(token_length, -1).astype(jnp.bfloat16),
        d_keys.reshape(2 * token_length, -1).astype(jnp.bfloat16),
        d_values.reshape(2 * token_length, -1).astype(jnp.bfloat16),
    )


def block_forward(
    token_rows,
    gradient_list,
    current_query_key_value,
    memory_key_value,
    memory_present,
    current_normed,
    current_normalized,
    current_inverse_deviation,
    query_key_value_weight,
    output_weight,
    scale_gain,
):
    token_length = token_rows.shape[0]
    mixed, probs, probs_b, query, keys, values = attend(
        current_query_key_value, memory_key_value, memory_present
    )
    block_output = (
        token_rows.astype(jnp.float32)
        + jnp.dot(mixed, output_weight, preferred_element_type=jnp.float32)
    ).astype(jnp.bfloat16)
    d_mixed = jnp.dot(gradient_list, output_weight.T, preferred_element_type=jnp.float32).astype(
        jnp.bfloat16
    )
    grad_wout = jnp.dot(mixed.T, gradient_list, preferred_element_type=jnp.float32)
    d_query, d_keys, d_values = attend_back(d_mixed, probs, probs_b, query, keys, values)
    d_own = jnp.concatenate([d_query, d_keys[token_length:], d_values[token_length:]], 1)
    memory_gradient = jnp.concatenate([d_keys[:token_length], d_values[:token_length]], 1)
    grad_wqkv = jnp.dot(current_normed.T, d_own, preferred_element_type=jnp.float32)
    normed_gradient = jnp.dot(d_own, query_key_value_weight.T, preferred_element_type=jnp.float32)
    gain_gradient = jnp.sum(normed_gradient * current_normalized, axis=0)
    grad_b = jnp.sum(normed_gradient, axis=0)
    normalized_gradient = normed_gradient * scale_gain
    row_gradient = current_inverse_deviation * (
        normalized_gradient
        - jnp.mean(normalized_gradient, axis=-1, keepdims=True)
        - current_normalized
        * jnp.mean(normalized_gradient * current_normalized, axis=-1, keepdims=True)
    )
    input_gradient = (gradient_list.astype(jnp.float32) + row_gradient).astype(jnp.bfloat16)
    return (
        block_output,
        input_gradient,
        memory_gradient,
        (grad_wqkv, grad_wout, gain_gradient, grad_b),
    )


def memory_contributions(prior_normed, prior_normalized, memory_gradient, query_key_value_weight):
    feature_width = prior_normed.shape[1]
    key_value_gradient = jnp.dot(
        prior_normed.T, memory_gradient, preferred_element_type=jnp.float32
    )
    normed_gradient = jnp.dot(
        memory_gradient,
        query_key_value_weight[:, feature_width:].T,
        preferred_element_type=jnp.float32,
    )
    return (
        key_value_gradient,
        jnp.sum(normed_gradient * prior_normalized, axis=0),
        jnp.sum(normed_gradient, axis=0),
    )


def on_device(
    layer_input, cotangent, layer_norm_gain, layer_norm_bias, query_key_value_weight, output_weight
):
    token_rows = layer_input[0]
    gradient_list = cotangent[0]
    feature_width = token_rows.shape[1]
    normed_rows, normalized_rows, inverse_deviation = apply_layer_norm(
        token_rows, layer_norm_gain, layer_norm_bias
    )
    query_key_value = jnp.dot(
        normed_rows, query_key_value_weight, preferred_element_type=jnp.float32
    ).astype(jnp.bfloat16)
    has_first = lax.axis_index(SEQ) > 0
    previous_token_rows = from_behind(token_rows, SEQ, 1)
    previous_normed_rows, previous_normalized, ignored_value = apply_layer_norm(
        previous_token_rows, layer_norm_gain, layer_norm_bias
    )
    kv_before = jnp.dot(
        previous_normed_rows,
        query_key_value_weight[:, feature_width:],
        preferred_element_type=jnp.float32,
    ).astype(jnp.bfloat16)
    block_output, input_gradient, memory_gradient, term_list = block_forward(
        token_rows,
        gradient_list,
        query_key_value,
        kv_before,
        has_first,
        normed_rows,
        normalized_rows,
        inverse_deviation,
        query_key_value_weight,
        output_weight,
        layer_norm_gain,
    )
    acc_qkv = term_list[0]
    acc_out = term_list[1]
    acc_gain = term_list[2]
    acc_bias = term_list[3]
    key_value_gradient, memory_gain, memory_bias = memory_contributions(
        previous_normed_rows, previous_normalized, memory_gradient, query_key_value_weight
    )
    acc_gain = acc_gain + memory_gain
    acc_bias = acc_bias + memory_bias
    combined = jnp.concatenate(
        [acc_qkv[:, :feature_width], acc_qkv[:, feature_width:] + key_value_gradient, acc_out], 1
    )
    seq_count = lax.axis_size(SEQ)
    slide_count = lax.axis_size("slide")
    factor = 1.0 / float(seq_count * slide_count * token_rows.shape[0]) ** 0.5
    gain_sum, bias_sum = (
        one_axis_at_a_time(acc_gain, SEQ_SLIDE),
        one_axis_at_a_time(acc_bias, SEQ_SLIDE),
    )
    shard = summed_rows(combined.astype(jnp.bfloat16), (("seq_0", "seq_1", "seq_2"), "seq_3"), 0)
    shard = over_copies(shard.astype(jnp.bfloat16), "slide").astype(jnp.float32)
    shard = shard * factor
    layer_output = block_output[None]
    input_grad = input_gradient[None]
    return (
        layer_output,
        input_grad,
        shard[:, : 3 * feature_width],
        shard[:, 3 * feature_width :],
        gain_sum * factor,
        bias_sum * factor,
    )


def solution(mesh):
    torus = Mesh(
        mesh.devices.reshape(4, 8, 2, 2, mesh.shape["slide"]),
        ("seq_0", "seq_1", "seq_2", "seq_3", "slide"),
    )
    return jax.shard_map(
        on_device,
        mesh=torus,
        in_specs=(P("slide", SEQ, None), P("slide", SEQ, None), P(), P(), P(), P()),
        out_specs=(
            P("slide", SEQ, None),
            P("slide", SEQ, None),
            P(SEQ, None),
            P(SEQ, None),
            P(),
            P(),
        ),
        check_vma=False,
    )
```

profile of v0, /device:TPU:8, one launch (start us, length us, event | category | flops | bytes accessed | tf_op | source)
XLA Modules:
  0.0 256.4 jit_solution(15733544273675283821)
XLA Ops:
  0.6 2.1 collective-permute-start
  5.1 3.4 %convolution_convert_fusion = bf16[256,2304]{1,0:T(8,128)(2,1)S(1)} fusion(bf16[768,2304]{1,0:T(8,128)(2,1)} %param.10, f32[256]{0:T(256)S(1)} %add_rsqrt_fusion, f32[256]{0:T(256)S(1)} %broadcast_multiply_fusion.5, f32[768]{0:T(1024)} %param.9, f32[768]{0:T(1024)} %param.8, bf16[1,256,768]{2,1,0:T(8,128)(2,1)} %param.6), kind=kOutput, calls=%fused_computation.11 | convolution fusion | flops 907739136 | bytes 5120000 | tf_op jit(solution)/shard_map/dot_general | solution.py:184
  12.2 2.3 collective-permute-done
  15.7 2.5 convolution_convert_fusion.1
  21.0 2.3 copy.59
  23.3 6.8 %fusion.96 = (f32[12,256]{1,0:T(8,128)}, f32[12,256,512]{2,1,0:T(8,128)}) fusion(pred[256,512]{1,0:T(8,128)(4,1)} %fusion.70, bf16[256,12,64]{0,2,1:T(8,128)(2,1)} %bitcast.78, bf16[512,12,64]{0,2,1:T(8,128)(2,1)} %bitcast.76), kind=kOutput, calls=%fused_computation.108 | convolution fusion | flops 207618560 | bytes 7614464 | tf_op jit(solution)/shard_map/sub | solution.py:86
  30.1 4.1 %fusion.38 = bf16[12,64,256]{2,1,0:T(8,128)(2,1)S(1)} fusion(bf16[512,12,64]{0,2,1:T(8,128)(2,1)S(1)} %bitcast.62, f32[12,256,512]{2,1,0:T(8,128)} %get-tuple-element.32, f32[12,256]{1,0:T(8,128)} %get-tuple-element.31), kind=kOutput, calls=%fused_computation.36 | convolution fusion | flops 204668928 | bytes 7483392 | tf_op jit(solution)/shard_map/hqk,khe->qhe/dot_general | solution.py:89
  34.7 1.7 fusion.31
  36.4 3.7 %fusion.97 = f32[12,256,512]{2,1,0:T(8,128)} fusion(bf16[256,12,64]{0,2,1:T(8,128)(2,1)S(1)} %bitcast.65, bf16[512,12,64]{0,2,1:T(8,128)(2,1)S(1)} %bitcast.63), kind=kOutput, calls=%fused_computation.109 | convolution fusion | flops 201326592 | bytes 7471104 | tf_op jit(solution)/shard_map/qhe,khe->hqk/dot_general | solution.py:97
  40.1 23.1 %fusion.34 = bf16[512,12,64]{0,2,1:T(8,128)(2,1)} fusion(bf16[256,12,64]{0,2,1:T(8,128)(2,1)} %bitcast.79, f32[12,256,512]{2,1,0:T(8,128)} %fusion.97, f32[12,256,512]{2,1,0:T(8,128)} %get-tuple-element.32, f32[12,256]{1,0:T(8,128)} %get-tuple-element.31), kind=kOutput, calls=%fused_computation.33 | convolution fusion | flops 212733440 | bytes 13774848 | tf_op jit(solution)/shard_map/hqk,qhe->khe/dot_general | solution.py:101
  63.2 25.5 %fusion.41 = bf16[12,64,256]{2,1,0:T(8,128)(2,1)} fusion(bf16[512,12,64]{0,2,1:T(8,128)(2,1)S(1)} %bitcast.77, f32[12,256,512]{2,1,0:T(8,128)} %fusion.97, f32[12,256,512]{2,1,0:T(8,128)} %get-tuple-element.32, f32[12,256]{1,0:T(8,128)S(1)} %copy-done.27), kind=kOutput, calls=%fused_computation.37 | convolution fusion | flops 212536832 | bytes 13774848 | tf_op jit(solution)/shard_map/hqk,khe->qhe/dot_general | solution.py:100
  88.7 2.1 fusion.94
  90.8 2.1 fusion.93
  96.9 2.5 fusion.4
  99.3 4.9 %concatenate.26 = bf16[64,2,6,1536]{3,2,1,0:T(8,128)(2,1)} reshape(bf16[768,1536]{1,0:T(8,128)(2,1)} %fusion.4) | data formatting | bytes 4718592 | tf_op jit(solution)/shard_map/concatenate | solution.py:219
  104.2 3.2 %concatenate.24 = bf16[64,2,6,768]{3,2,1,0:T(8,128)(2,1)} reshape(bf16[768,768]{1,0:T(8,128)(2,1)} %slice.95) | data formatting | bytes 2359296 | tf_op jit(solution)/shard_map/concatenate | solution.py:219
  107.4 3.9 %maximum_bitcast_fusion = bf16[2,64,6,3072]{3,2,0,1:T(8,128)(2,1)S(1)} fusion(bf16[64,2,6,768]{3,2,1,0:T(8,128)(2,1)S(1)} %copy.62, bf16[64,2,6,1536]{3,2,1,0:T(8,128)(2,1)} %concatenate.26, bf16[64,2,6,768]{3,2,1,0:T(8,128)(2,1)} %concatenate.24), kind=kLoop, calls=%fused_computation.2 | loop fusion | flops 14155776 | bytes 9437184 | tf_op jit(solution)/shard_map/transpose | solution.py:27
  111.4 2.6 %copy.63 = bf16[2,64,6,3072]{3,1,2,0:T(8,128)(2,1)S(1)} copy(bf16[2,64,6,3072]{3,2,0,1:T(8,128)(2,1)S(1)} %maximum_bitcast_fusion) | data formatting | bytes 9437184 | tf_op jit(solution)/shard_map/transpose | solution.py:27
  114.0 8.6 %all_to_all.15 = bf16[2,64,6,3072]{3,1,2,0:T(8,128)(2,1)} all-to-all(bf16[2,64,6,3072]{3,1,2,0:T(8,128)(2,1)S(1)} %copy.63), channel_id=1, replica_groups=mesh['seq_0'=4,'seq_1'=8,'seq_2'=2,'seq_3'=2,'slide'=2] {'seq_3'}, dimensions={0} | all-to-all | bytes 9437184 | tf_op jit(solution)/shard_map/all_to_all | solution.py:32
  122.6 5.5 %reduce_sum.149 = bf16[64,6,3072]{2,0,1:T(8,128)(2,1)} reduce(bf16[2,64,6,3072]{3,1,2,0:T(8,128)(2,1)} %all_to_all.15, bf16[]{:T(256)} %constant.51.clone.1), dimensions={0}, to_apply=%region_9.10 | reduce | flops 1179648 | bytes 7077890 | tf_op jit(solution)/shard_map/reduce_sum | solution.py:33
  128.1 4.6 %copy.64 = bf16[64,6,3072]{2,1,0:T(8,128)(2,1)} copy(bf16[64,6,3072]{2,0,1:T(8,128)(2,1)} %reduce_sum.149) | data formatting | bytes 4718592 | tf_op jit(solution)/shard_map/reduce_sum | solution.py:33
  132.8 11.6 %all-to-all-start.1 = ((bf16[64,6,3072]{2,1,0:T(8,128)(2,1)}), bf16[64,6,3072]{2,1,0:T(8,128)(2,1)}, u32[]{:S(2)}, u32[]{:S(2)}) async-start(bf16[64,6,3072]{2,1,0:T(8,128)(2,1)} %copy.64), calls=%async_computation.1 | async-start | bytes 6291456 | tf_op jit(solution)/shard_map/all_to_all | solution.py:40
  144.5 2.7 %fusion.91 = (f32[768]{0:T(1024)S(1)}, f32[768]{0:T(1024)S(1)}) fusion(f32[256]{0:T(256)} %copy-done.22, f32[256]{0:T(256)S(1)} %copy-done.21, bf16[256,768]{1,0:T(8,128)(2,1)S(1)} %collective-permute-done, bf16[768,2304]{1,0:T(8,128)(2,1)} %param.10, bf16[256,768]{0,1:T(8,128)(2,1)S(1)} %bitcast.73, bf16[256,768]{0,1:T(8,128)(2,1)S(1)} %bitcast.75), kind=kOutput, calls=%fused_computation.103 | convolution fusion | flops 606730752 | bytes 3547136 | tf_op jit(solution)/shard_map/dot_general | solution.py:163
  147.6 1.9 fusion.65
  149.5 9.7 %all-reduce.1 = (f32[768]{0:T(1024)S(1)}, f32[768]{0:T(1024)S(1)}) all-reduce(f32[768]{0:T(1024)S(1)} %add.86, f32[768]{0:T(1024)S(1)} %add.87), channel_id=1, replica_groups=mesh['seq_0'=4,'seq_1'=8,'seq_2'=2,'seq_3'=2,'slide'=2] {'seq_0'}, use_global_device_ids=true, to_apply=%region_14.15 | all-reduce | flops 1536 | bytes 12288 | tf_op jit(solution)/shard_map/psum | solution.py:21
  159.2 65.0 %all-reduce = (f32[768]{0:T(1024)S(1)}, f32[768]{0:T(1024)S(1)}) all-reduce(f32[768]{0:T(1024)S(1)} %get-tuple-element.14, f32[768]{0:T(1024)S(1)} %get-tuple-element.15), channel_id=1, replica_groups=mesh['seq_0'=4,'seq_1'=8,'seq_2'=2,'seq_3'=2,'slide'=2] {'seq_1'}, use_global_device_ids=true, to_apply=%region_15.16 | all-reduce | flops 1536 | bytes 12288 | tf_op jit(solution)/shard_map/psum | solution.py:21
  224.2 5.0 %all-reduce.4 = (f32[768]{0:T(1024)S(1)}, f32[768]{0:T(1024)S(1)}) all-reduce(f32[768]{0:T(1024)S(1)} %get-tuple-element.12, f32[768]{0:T(1024)S(1)} %get-tuple-element.13), channel_id=1, replica_groups=mesh['seq_0'=4,'seq_1'=8,'seq_2'=2,'seq_3'=2,'slide'=2] {'seq_2'}, use_global_device_ids=true, to_apply=%region_16.17 | all-reduce | flops 1536 | bytes 12288 | tf_op jit(solution)/shard_map/psum | solution.py:21
  229.2 2.5 all-reduce.3
  231.7 6.5 %all-reduce.2 = (f32[768]{0:T(1024)S(1)}, f32[768]{0:T(1024)S(1)}) all-reduce(f32[768]{0:T(1024)S(1)} %get-tuple-element.18, f32[768]{0:T(1024)S(1)} %get-tuple-element.19), channel_id=1, replica_groups=mesh['seq_0'=4,'seq_1'=8,'seq_2'=2,'seq_3'=2,'slide'=2] {'slide'}, use_global_device_ids=true, to_apply=%region_18.19 | all-reduce | flops 1536 | bytes 12288 | tf_op jit(solution)/shard_map/psum | solution.py:21
  241.8 2.5 reduce_sum.150
  245.0 4.3 %all-to-all-start.2 = ((bf16[2,6,3072]{2,1,0:T(8,128)(2,1)}), bf16[2,6,3072]{2,1,0:T(8,128)(2,1)S(1)}, u32[]{:S(2)}, u32[]{:S(2)}) async-start(bf16[2,6,3072]{2,1,0:T(8,128)(2,1)} %broadcast_in_dim.27), calls=%async_computation.2 | async-start | bytes 196608 | tf_op jit(solution)/shard_map/all_to_all | solution.py:46
  250.5 4.5 %all-to-all-done.2 = bf16[2,6,3072]{2,1,0:T(8,128)(2,1)S(1)} async-done(((bf16[2,6,3072]{2,1,0:T(8,128)(2,1)}), bf16[2,6,3072]{2,1,0:T(8,128)(2,1)S(1)}, u32[]{:S(2)}, u32[]{:S(2)}) %all-to-all-start.2) | async-done | bytes 73760 | tf_op jit(solution)/shard_map/all_to_all | solution.py:46
  (93 shorter events, 21.5 us)
Async XLA Ops:
  0.6 8.0 %copy-start = (bf16[768,768]{1,0:T(8,128)(2,1)S(1)}, bf16[768,768]{1,0:T(8,128)(2,1)}, u32[]{:S(2)}) copy-start(bf16[768,768]{1,0:T(8,128)(2,1)} %param.11) | copy-start | bytes 3538948
  0.6 13.8 %collective-permute-start = (bf16[256,768]{1,0:T(8,128)(2,1)}, bf16[256,768]{1,0:T(8,128)(2,1)S(1)}, u32[]{:S(2)}, u32[]{:S(2)}) collective-permute-start(bf16[256,768]{1,0:T(8,128)(2,1)} %bitcast.61), channel_id=1, source_target_pairs={{0,2},{2,4},{4,6},{6,8},{8,10},{10,12},{12,14},{14,16},{16,18},{18... | collective-permute-start | bytes 1179656 | tf_op jit(solution)/shard_map/ppermute | solution.py:16
  5.1 3.5 %copy-start.2 = (bf16[1,256,768]{2,1,0:T(8,128)(2,1)S(1)}, bf16[1,256,768]{2,1,0:T(8,128)(2,1)}, u32[]{:S(2)}) copy-start(bf16[1,256,768]{2,1,0:T(8,128)(2,1)} %param.7) | copy-start | bytes 1179652
  8.5 7.2 %copy-start.17 = (f32[768]{0:T(1024)S(1)}, f32[768]{0:T(1024)}, u32[]{:S(2)}) copy-start(f32[768]{0:T(1024)} %param.8) | copy-start | bytes 9220
  8.5 7.2 %copy-start.18 = (f32[768]{0:T(1024)S(1)}, f32[768]{0:T(1024)}, u32[]{:S(2)}) copy-start(f32[768]{0:T(1024)} %param.9) | copy-start | bytes 9220
  14.6 0.6 copy-start.19
  15.2 0.6 copy-start.22
  30.1 4.6 %copy-start.25 = (f32[12,256,512]{2,1,0:T(8,128)S(1)}, f32[12,256,512]{2,1,0:T(8,128)}, u32[]{:S(2)}) copy-start(f32[12,256,512]{2,1,0:T(8,128)} %get-tuple-element.32) | copy-start | bytes 18874372
  30.1 4.6 %copy-start.26 = (f32[12,256]{1,0:T(8,128)S(1)}, f32[12,256]{1,0:T(8,128)}, u32[]{:S(2)}) copy-start(f32[12,256]{1,0:T(8,128)} %get-tuple-element.31) | copy-start | bytes 36868
  34.2 58.8 %copy-start.4 = (bf16[12,64,256]{2,1,0:T(8,128)(2,1)}, bf16[12,64,256]{2,1,0:T(8,128)(2,1)S(1)}, u32[]{:S(2)}) copy-start(bf16[12,64,256]{2,1,0:T(8,128)(2,1)S(1)} %fusion.38) | copy-start | bytes 1179652
  40.1 23.1 %copy-start.14 = (bf16[512,768]{0,1:T(8,128)(2,1)S(1)}, bf16[512,768]{0,1:T(8,128)(2,1)}, u32[]{:S(2)}) copy-start(bf16[512,768]{0,1:T(8,128)(2,1)} %copy.59) | copy-start | bytes 2359300
  40.1 23.1 %copy-start.27 = (f32[12,256]{1,0:T(8,128)S(1)}, f32[12,256]{1,0:T(8,128)}, u32[]{:S(2)}) copy-start(f32[12,256]{1,0:T(8,128)} %get-tuple-element.31) | copy-start | bytes 36868
  90.8 3.5 %copy-start.1 = (bf16[1,256,768]{2,1,0:T(8,128)(2,1)S(1)}, bf16[1,256,768]{2,1,0:T(8,128)(2,1)}, u32[]{:S(2)}) copy-start(bf16[1,256,768]{2,1,0:T(8,128)(2,1)} %param.6) | copy-start | bytes 1179652
  93.1 1.2 copy-start.6
  93.1 1.2 copy-start.8
  93.1 1.2 copy-start.15
  94.3 2.5 copy-start.10
  94.3 2.5 copy-start.12
  94.3 2.5 copy-start.20
  94.4 2.5 copy-start.23
  132.8 11.6 %copy-start.11 = (bf16[256,12,64]{0,2,1:T(8,128)(2,1)S(1)}, bf16[256,12,64]{0,2,1:T(8,128)(2,1)}, u32[]{:S(2)}) copy-start(bf16[256,12,64]{0,2,1:T(8,128)(2,1)} %get-tuple-element.27) | copy-start | bytes 1179652
  132.8 11.7 %copy-start.13 = (bf16[256,12,64]{0,2,1:T(8,128)(2,1)S(1)}, bf16[256,12,64]{0,2,1:T(8,128)(2,1)}, u32[]{:S(2)}) copy-start(bf16[256,12,64]{0,2,1:T(8,128)(2,1)} %get-tuple-element.25) | copy-start | bytes 1179652
  132.8 11.7 %copy-start.21 = (f32[256]{0:T(256)S(1)}, f32[256]{0:T(256)}, u32[]{:S(2)}) copy-start(f32[256]{0:T(256)} %copy-done.19) | copy-start | bytes 3076
  132.8 109.0 %all-to-all-start.1 = ((bf16[64,6,3072]{2,1,0:T(8,128)(2,1)}), bf16[64,6,3072]{2,1,0:T(8,128)(2,1)}, u32[]{:S(2)}, u32[]{:S(2)}) async-start(bf16[64,6,3072]{2,1,0:T(8,128)(2,1)} %copy.64), calls=%async_computation.1 | async-start | bytes 6291456 | tf_op jit(solution)/shard_map/all_to_all | solution.py:40
  144.5 2.7 %copy-start.7 = (bf16[256,12,64]{0,2,1:T(8,128)(2,1)S(1)}, bf16[256,12,64]{0,2,1:T(8,128)(2,1)}, u32[]{:S(2)}) copy-start(bf16[256,12,64]{0,2,1:T(8,128)(2,1)} %get-tuple-element.28) | copy-start | bytes 1179652
  144.5 2.7 %copy-start.9 = (bf16[256,12,64]{0,2,1:T(8,128)(2,1)S(1)}, bf16[256,12,64]{0,2,1:T(8,128)(2,1)}, u32[]{:S(2)}) copy-start(bf16[256,12,64]{0,2,1:T(8,128)(2,1)} %get-tuple-element.26) | copy-start | bytes 1179652
  144.5 2.7 %copy-start.16 = (bf16[12,64,256]{2,1,0:T(8,128)(2,1)S(1)}, bf16[12,64,256]{2,1,0:T(8,128)(2,1)}, u32[]{:S(2)}) copy-start(bf16[12,64,256]{2,1,0:T(8,128)(2,1)} %fusion.41) | copy-start | bytes 1179652
  144.5 3.1 %copy-start.24 = (bf16[768,2304]{1,0:T(8,128)(2,1)S(1)}, bf16[768,2304]{1,0:T(8,128)(2,1)}, u32[]{:S(2)}) copy-start(bf16[768,2304]{1,0:T(8,128)(2,1)} %param.10) | copy-start | bytes 10616836
  147.6 93.2 %copy-start.3 = (bf16[1,256,768]{2,1,0:T(8,128)(2,1)S(1)}, bf16[1,256,768]{2,1,0:T(8,128)(2,1)}, u32[]{:S(2)}) copy-start(bf16[1,256,768]{2,1,0:T(8,128)(2,1)} %param.7) | copy-start | bytes 1179652
  149.5 99.8 %copy-start.5 = (bf16[12,64,256]{2,1,0:T(8,128)(2,1)S(1)}, bf16[12,64,256]{2,1,0:T(8,128)(2,1)}, u32[]{:S(2)}) copy-start(bf16[12,64,256]{2,1,0:T(8,128)(2,1)} %copy-done.4) | copy-start | bytes 1179652
  245.0 10.1 %all-to-all-start.2 = ((bf16[2,6,3072]{2,1,0:T(8,128)(2,1)}), bf16[2,6,3072]{2,1,0:T(8,128)(2,1)S(1)}, u32[]{:S(2)}, u32[]{:S(2)}) async-start(bf16[2,6,3072]{2,1,0:T(8,128)(2,1)} %broadcast_in_dim.27), calls=%async_computation.2 | async-start | bytes 196608 | tf_op jit(solution)/shard_map/all_to_all | solution.py:46
where the time goes:
time: 257 us; the launch traced here: 256 us
  blocking collectives  97.3 us (38%)
  matrix products  81.4 us (32%)
  local copies, waits for them, and re-layouts  30.1 us (12%)
  other arithmetic  21.6 us (8%)
  starting transfers between devices  18 us (7%)
  waiting for transfers between devices  6.83 us (3%)
    psum x5, blocking collectives, one_axis_at_a_time(): shard = lax.psum(shard, axis)  88.7 us
    dot_general x1, matrix products, attend_back(): jnp.einsum('hqk,khe->qhe', d_scores_b, keys, preferred_element_type=jnp.f...  25.5 us
    dot_general x1, matrix products, attend_back(): jnp.einsum('hqk,qhe->khe', d_scores_b, query, preferred_element_type=jnp....  23.1 us
    all_to_all x1, starting transfers between devices, summed_rows(): lax.all_to_all(own.astype(jnp.bfloat16), far, 0, 0, tiled=True)  11.6 us
    all_to_all x1, blocking collectives, sent_and_summed(): lax.all_to_all(cut_along(shard, dim, peers), axis, 0, 0, tiled=True)  8.61 us
    concatenate x2, local copies, waits for them, and re-layouts, on_device(): jnp.concatenate([acc_qkv[:, :feature_width], acc_qkv[:, feature_width:] +...  8.11 us
    sub x1, matrix products, attend(): weights = jnp.exp(scores - top)  6.78 us
    reduce_sum x1, other arithmetic, sent_and_summed(): return jnp.sum(pieces.astype(jnp.float32), axis=0)  5.53 us
  transfers between devices with their start and end apart: 3, of which 2 were waited for; matrix products, arithmetic and copies ran while one was open for 7% of the time, Pallas kernels for 0%

commit v1 on v0

--- a/solution.py
+++ b/solution.py
@@ -18,7 +18,7 @@
 
 def one_axis_at_a_time(shard, axes):
     for axis in axes:
-        shard = lax.psum(shard, axis)
+        shard = jnp.sum(lax.all_gather(shard, axis), axis=0)
     return shard
 
 

time: 257 us -> 314 us (1.22)
  blocking collectives: 97.3 us -> 152 us
    all_gather x0 -> x10, blocking collectives: none -> 144 us  [one_axis_at_a_time(): shard = jnp.sum(lax.all_gather(shard, axis), axis=0)]
    psum x5 -> x0, blocking collectives: 88.7 us -> none  [one_axis_at_a_time(): shard = lax.psum(shard, axis)]
where the time goes in v1:
time: 314 us; the launch traced here: 313 us
  blocking collectives  152 us (48%)
  matrix products  82.1 us (26%)
  local copies, waits for them, and re-layouts  29.8 us (9%)
  other arithmetic  22.5 us (7%)
  starting transfers between devices  18 us (6%)
  waiting for transfers between devices  6.83 us (2%)
    all_gather x10, blocking collectives, one_axis_at_a_time(): shard = jnp.sum(lax.all_gather(shard, axis), axis=0)  144 us
    dot_general x1, matrix products, attend_back(): jnp.einsum('hqk,khe->qhe', d_scores_b, keys, preferred_element_type=jnp.f...  25.5 us
    dot_general x1, matrix products, attend_back(): jnp.einsum('hqk,qhe->khe', d_scores_b, query, preferred_element_type=jnp....  23.1 us
    all_to_all x1, starting transfers between devices, summed_rows(): lax.all_to_all(own.astype(jnp.bfloat16), far, 0, 0, tiled=True)  11.6 us
    all_to_all x1, blocking collectives, sent_and_summed(): lax.all_to_all(cut_along(shard, dim, peers), axis, 0, 0, tiled=True)  8.61 us
    concatenate x2, local copies, waits for them, and re-layouts, on_device(): jnp.concatenate([acc_qkv[:, :feature_width], acc_qkv[:, feature_width:] +...  8.11 us
    sub x1, matrix products, attend(): weights = jnp.exp(scores - top)  6.78 us
  transfers between devices with their start and end apart: 3, of which 2 were waited for; matrix products, arithmetic and copies ran while one was open for 7% of the time, Pallas kernels for 0%

profile of v1, /device:TPU:8, one launch (start us, length us, event | category | flops | bytes accessed | tf_op | source)
XLA Modules:
  0.0 312.8 jit_solution(17794136613447640525)
XLA Ops:
  5.1 3.4 %convolution_convert_fusion = bf16[256,2304]{1,0:T(8,128)(2,1)S(1)} fusion(bf16[768,2304]{1,0:T(8,128)(2,1)} %param.10, f32[256]{0:T(256)S(1)} %add_rsqrt_fusion, f32[256]{0:T(256)S(1)} %broadcast_multiply_fusion.5, f32[768]{0:T(1024)} %param.9, f32[768]{0:T(1024)} %param.8, bf16[1,256,768]{2,1,0:T(8,128)(2,1)} %param.6), kind=kOutput, calls=%fused_computation.11 | convolution fusion | flops 907739136 | bytes 5120000 | tf_op jit(solution)/shard_map/dot_general | solution.py:184
  12.2 2.3 collective-permute-done
  15.7 2.5 convolution_convert_fusion.1
  21.0 2.3 copy.59
  23.3 6.8 %fusion.96 = (f32[12,256]{1,0:T(8,128)}, f32[12,256,512]{2,1,0:T(8,128)}) fusion(pred[256,512]{1,0:T(8,128)(4,1)} %fusion.70, bf16[256,12,64]{0,2,1:T(8,128)(2,1)} %bitcast.78, bf16[512,12,64]{0,2,1:T(8,128)(2,1)} %bitcast.76), kind=kOutput, calls=%fused_computation.108 | convolution fusion | flops 207618560 | bytes 7614464 | tf_op jit(solution)/shard_map/sub | solution.py:86
  30.1 4.1 %fusion.38 = bf16[12,64,256]{2,1,0:T(8,128)(2,1)S(1)} fusion(bf16[512,12,64]{0,2,1:T(8,128)(2,1)S(1)} %bitcast.62, f32[12,256,512]{2,1,0:T(8,128)} %get-tuple-element.22, f32[12,256]{1,0:T(8,128)} %get-tuple-element.21), kind=kOutput, calls=%fused_computation.36 | convolution fusion | flops 204668928 | bytes 7483392 | tf_op jit(solution)/shard_map/hqk,khe->qhe/dot_general | solution.py:89
  36.4 3.7 %fusion.97 = f32[12,256,512]{2,1,0:T(8,128)} fusion(bf16[256,12,64]{0,2,1:T(8,128)(2,1)S(1)} %bitcast.65, bf16[512,12,64]{0,2,1:T(8,128)(2,1)S(1)} %bitcast.63), kind=kOutput, calls=%fused_computation.109 | convolution fusion | flops 201326592 | bytes 7471104 | tf_op jit(solution)/shard_map/qhe,khe->hqk/dot_general | solution.py:97
  40.1 23.1 %fusion.34 = bf16[512,12,64]{0,2,1:T(8,128)(2,1)} fusion(bf16[256,12,64]{0,2,1:T(8,128)(2,1)} %bitcast.79, f32[12,256,512]{2,1,0:T(8,128)} %fusion.97, f32[12,256,512]{2,1,0:T(8,128)} %get-tuple-element.22, f32[12,256]{1,0:T(8,128)} %get-tuple-element.21), kind=kOutput, calls=%fused_computation.33 | convolution fusion | flops 212733440 | bytes 13774848 | tf_op jit(solution)/shard_map/hqk,qhe->khe/dot_general | solution.py:101
  63.2 25.5 %fusion.41 = bf16[12,64,256]{2,1,0:T(8,128)(2,1)} fusion(bf16[512,12,64]{0,2,1:T(8,128)(2,1)S(1)} %bitcast.77, f32[12,256,512]{2,1,0:T(8,128)} %fusion.97, f32[12,256,512]{2,1,0:T(8,128)} %get-tuple-element.22, f32[12,256]{1,0:T(8,128)S(1)} %copy-done.27), kind=kOutput, calls=%fused_computation.37 | convolution fusion | flops 212536832 | bytes 13774848 | tf_op jit(solution)/shard_map/hqk,khe->qhe/dot_general | solution.py:100
  88.7 2.1 fusion.94
  90.8 2.1 fusion.93
  96.9 2.5 fusion.4
  99.3 4.9 %concatenate.26 = bf16[64,2,6,1536]{3,2,1,0:T(8,128)(2,1)} reshape(bf16[768,1536]{1,0:T(8,128)(2,1)} %fusion.4) | data formatting | bytes 4718592 | tf_op jit(solution)/shard_map/concatenate | solution.py:219
  104.2 3.2 %concatenate.24 = bf16[64,2,6,768]{3,2,1,0:T(8,128)(2,1)} reshape(bf16[768,768]{1,0:T(8,128)(2,1)} %slice.95) | data formatting | bytes 2359296 | tf_op jit(solution)/shard_map/concatenate | solution.py:219
  107.4 3.9 %maximum_bitcast_fusion = bf16[2,64,6,3072]{3,2,0,1:T(8,128)(2,1)S(1)} fusion(bf16[64,2,6,768]{3,2,1,0:T(8,128)(2,1)S(1)} %copy.62, bf16[64,2,6,1536]{3,2,1,0:T(8,128)(2,1)} %concatenate.26, bf16[64,2,6,768]{3,2,1,0:T(8,128)(2,1)} %concatenate.24), kind=kLoop, calls=%fused_computation.2 | loop fusion | flops 14155776 | bytes 9437184 | tf_op jit(solution)/shard_map/transpose | solution.py:27
  111.4 2.6 copy.63
  114.0 8.6 %all_to_all.15 = bf16[2,64,6,3072]{3,1,2,0:T(8,128)(2,1)} all-to-all(bf16[2,64,6,3072]{3,1,2,0:T(8,128)(2,1)S(1)} %copy.63), channel_id=1, replica_groups=mesh['seq_0'=4,'seq_1'=8,'seq_2'=2,'seq_3'=2,'slide'=2] {'seq_3'}, dimensions={0} | all-to-all | bytes 9437184 | tf_op jit(solution)/shard_map/all_to_all | solution.py:32
  122.6 5.5 %reduce_sum.239 = bf16[64,6,3072]{2,0,1:T(8,128)(2,1)} reduce(bf16[2,64,6,3072]{3,1,2,0:T(8,128)(2,1)} %all_to_all.15, bf16[]{:T(256)} %constant.51.clone.1), dimensions={0}, to_apply=%region_9.10 | reduce | flops 1179648 | bytes 7077890 | tf_op jit(solution)/shard_map/reduce_sum | solution.py:33
  128.1 4.6 %copy.64 = bf16[64,6,3072]{2,1,0:T(8,128)(2,1)} copy(bf16[64,6,3072]{2,0,1:T(8,128)(2,1)} %reduce_sum.239) | data formatting | bytes 4718592 | tf_op jit(solution)/shard_map/reduce_sum | solution.py:33
  132.8 11.6 %all-to-all-start.1 = ((bf16[64,6,3072]{2,1,0:T(8,128)(2,1)}), bf16[64,6,3072]{2,1,0:T(8,128)(2,1)}, u32[]{:S(2)}, u32[]{:S(2)}) async-start(bf16[64,6,3072]{2,1,0:T(8,128)(2,1)} %copy.64), calls=%async_computation.1 | async-start | bytes 6291456 | tf_op jit(solution)/shard_map/all_to_all | solution.py:40
  144.5 3.3 %fusion.91 = (f32[768]{0:T(1024)}, f32[768]{0:T(1024)S(1)}) fusion(f32[256]{0:T(256)} %copy-done.22, f32[256]{0:T(256)S(1)} %copy-done.21, bf16[256,768]{1,0:T(8,128)(2,1)S(1)} %collective-permute-done, bf16[768,2304]{1,0:T(8,128)(2,1)} %param.10, bf16[256,768]{0,1:T(8,128)(2,1)S(1)} %bitcast.73, bf16[256,768]{0,1:T(8,128)(2,1)S(1)} %bitcast.75), kind=kOutput, calls=%fused_computation.103 | convolution fusion | flops 606730752 | bytes 3547136 | tf_op jit(solution)/shard_map/dot_general | solution.py:163
  149.8 12.4 %all-gather.10 = f32[4,1,768]{2,1,0:T(1,128)S(1)} all-gather(f32[1,1,768]{2,1,0:T(1,128)S(1)} %reshape.149), channel_id=2, replica_groups=mesh['seq_0'=4,'seq_1'=8,'seq_2'=2,'seq_3'=2,'slide'=2] {'seq_0'}, dimensions={0}, use_global_device_ids=true | all-gather | bytes 15360 | tf_op jit(solution)/shard_map/all_gather | solution.py:21
  162.2 70.0 %all-gather.11 = f32[8,1,768]{2,1,0:T(1,128)S(1)} all-gather(f32[1,1,768]{2,1,0:T(1,128)S(1)} %reshape.151), channel_id=3, replica_groups=mesh['seq_0'=4,'seq_1'=8,'seq_2'=2,'seq_3'=2,'slide'=2] {'seq_1'}, dimensions={0}, use_global_device_ids=true | all-gather | bytes 27648 | tf_op jit(solution)/shard_map/all_gather | solution.py:21
  232.2 5.3 %all-gather.12 = f32[2,1,768]{2,1,0:T(1,128)S(1)} all-gather(f32[1,1,768]{2,1,0:T(1,128)S(1)} %reshape.153), channel_id=4, replica_groups=mesh['seq_0'=4,'seq_1'=8,'seq_2'=2,'seq_3'=2,'slide'=2] {'seq_2'}, dimensions={0}, use_global_device_ids=true | all-gather | bytes 9216 | tf_op jit(solution)/shard_map/all_gather | solution.py:21
  239.3 5.8 %all-gather.14 = f32[2,1,768]{2,1,0:T(1,128)S(1)} all-gather(f32[1,1,768]{2,1,0:T(1,128)S(1)} %reshape.157), channel_id=6, replica_groups=mesh['seq_0'=4,'seq_1'=8,'seq_2'=2,'seq_3'=2,'slide'=2] {'slide'}, dimensions={0}, use_global_device_ids=true | all-gather | bytes 9216 | tf_op jit(solution)/shard_map/all_gather | solution.py:21
  245.9 12.1 %all-gather.15 = f32[4,1,768]{2,1,0:T(1,128)S(1)} all-gather(f32[1,1,768]{2,1,0:T(1,128)S(1)} %reshape.159), channel_id=7, replica_groups=mesh['seq_0'=4,'seq_1'=8,'seq_2'=2,'seq_3'=2,'slide'=2] {'seq_0'}, dimensions={0}, use_global_device_ids=true | all-gather | bytes 15360 | tf_op jit(solution)/shard_map/all_gather | solution.py:21
  258.1 24.4 %all-gather.16 = f32[8,1,768]{2,1,0:T(1,128)S(1)} all-gather(f32[1,1,768]{2,1,0:T(1,128)S(1)} %reshape.161), channel_id=8, replica_groups=mesh['seq_0'=4,'seq_1'=8,'seq_2'=2,'seq_3'=2,'slide'=2] {'seq_1'}, dimensions={0}, use_global_device_ids=true | all-gather | bytes 27648 | tf_op jit(solution)/shard_map/all_gather | solution.py:21
  282.5 4.3 %all-gather.17 = f32[2,1,768]{2,1,0:T(1,128)S(1)} all-gather(f32[1,1,768]{2,1,0:T(1,128)S(1)} %reshape.163), channel_id=9, replica_groups=mesh['seq_0'=4,'seq_1'=8,'seq_2'=2,'seq_3'=2,'slide'=2] {'seq_2'}, dimensions={0}, use_global_device_ids=true | all-gather | bytes 9216 | tf_op jit(solution)/shard_map/all_gather | solution.py:21
  288.7 5.8 %all-gather.19 = f32[2,1,768]{2,1,0:T(1,128)S(1)} all-gather(f32[1,1,768]{2,1,0:T(1,128)S(1)} %reshape.167), channel_id=11, replica_groups=mesh['seq_0'=4,'seq_1'=8,'seq_2'=2,'seq_3'=2,'slide'=2] {'slide'}, dimensions={0}, use_global_device_ids=true | all-gather | bytes 9216 | tf_op jit(solution)/shard_map/all_gather | solution.py:21
  298.2 2.5 reduce_sum.240
  301.4 4.3 %all-to-all-start.2 = ((bf16[2,6,3072]{2,1,0:T(8,128)(2,1)}), bf16[2,6,3072]{2,1,0:T(8,128)(2,1)S(1)}, u32[]{:S(2)}, u32[]{:S(2)}) async-start(bf16[2,6,3072]{2,1,0:T(8,128)(2,1)} %broadcast_in_dim.27), calls=%async_computation.2 | async-start | bytes 196608 | tf_op jit(solution)/shard_map/all_to_all | solution.py:46
  306.9 4.5 %all-to-all-done.2 = bf16[2,6,3072]{2,1,0:T(8,128)(2,1)S(1)} async-done(((bf16[2,6,3072]{2,1,0:T(8,128)(2,1)}), bf16[2,6,3072]{2,1,0:T(8,128)(2,1)S(1)}, u32[]{:S(2)}, u32[]{:S(2)}) %all-to-all-start.2) | async-done | bytes 73760 | tf_op jit(solution)/shard_map/all_to_all | solution.py:46
  (118 shorter events, 31.4 us)
Async XLA Ops:
  0.6 8.0 %copy-start = (bf16[768,768]{1,0:T(8,128)(2,1)S(1)}, bf16[768,768]{1,0:T(8,128)(2,1)}, u32[]{:S(2)}) copy-start(bf16[768,768]{1,0:T(8,128)(2,1)} %param.11) | copy-start | bytes 3538948
  0.6 13.8 %collective-permute-start = (bf16[256,768]{1,0:T(8,128)(2,1)}, bf16[256,768]{1,0:T(8,128)(2,1)S(1)}, u32[]{:S(2)}, u32[]{:S(2)}) collective-permute-start(bf16[256,768]{1,0:T(8,128)(2,1)} %bitcast.61), channel_id=1, source_target_pairs={{0,2},{2,4},{4,6},{6,8},{8,10},{10,12},{12,14},{14,16},{16,18},{18... | collective-permute-start | bytes 1179656 | tf_op jit(solution)/shard_map/ppermute | solution.py:16
  5.1 3.5 %copy-start.2 = (bf16[1,256,768]{2,1,0:T(8,128)(2,1)S(1)}, bf16[1,256,768]{2,1,0:T(8,128)(2,1)}, u32[]{:S(2)}) copy-start(bf16[1,256,768]{2,1,0:T(8,128)(2,1)} %param.7) | copy-start | bytes 1179652
  8.5 7.2 %copy-start.17 = (f32[768]{0:T(1024)S(1)}, f32[768]{0:T(1024)}, u32[]{:S(2)}) copy-start(f32[768]{0:T(1024)} %param.8) | copy-start | bytes 9220
  8.5 7.2 %copy-start.18 = (f32[768]{0:T(1024)S(1)}, f32[768]{0:T(1024)}, u32[]{:S(2)}) copy-start(f32[768]{0:T(1024)} %param.9) | copy-start | bytes 9220
  14.6 0.6 copy-start.19
  15.2 0.6 copy-start.22
  30.1 4.6 %copy-start.25 = (f32[12,256,512]{2,1,0:T(8,128)S(1)}, f32[12,256,512]{2,1,0:T(8,128)}, u32[]{:S(2)}) copy-start(f32[12,256,512]{2,1,0:T(8,128)} %get-tuple-element.22) | copy-start | bytes 18874372
  30.1 4.6 %copy-start.26 = (f32[12,256]{1,0:T(8,128)S(1)}, f32[12,256]{1,0:T(8,128)}, u32[]{:S(2)}) copy-start(f32[12,256]{1,0:T(8,128)} %get-tuple-element.21) | copy-start | bytes 36868
  34.2 58.8 %copy-start.4 = (bf16[12,64,256]{2,1,0:T(8,128)(2,1)}, bf16[12,64,256]{2,1,0:T(8,128)(2,1)S(1)}, u32[]{:S(2)}) copy-start(bf16[12,64,256]{2,1,0:T(8,128)(2,1)S(1)} %fusion.38) | copy-start | bytes 1179652
  40.1 23.1 %copy-start.14 = (bf16[512,768]{0,1:T(8,128)(2,1)S(1)}, bf16[512,768]{0,1:T(8,128)(2,1)}, u32[]{:S(2)}) copy-start(bf16[512,768]{0,1:T(8,128)(2,1)} %copy.59) | copy-start | bytes 2359300
  40.1 23.1 %copy-start.27 = (f32[12,256]{1,0:T(8,128)S(1)}, f32[12,256]{1,0:T(8,128)}, u32[]{:S(2)}) copy-start(f32[12,256]{1,0:T(8,128)} %get-tuple-element.21) | copy-start | bytes 36868
  90.8 3.5 %copy-start.1 = (bf16[1,256,768]{2,1,0:T(8,128)(2,1)S(1)}, bf16[1,256,768]{2,1,0:T(8,128)(2,1)}, u32[]{:S(2)}) copy-start(bf16[1,256,768]{2,1,0:T(8,128)(2,1)} %param.6) | copy-start | bytes 1179652
  93.1 1.2 copy-start.6
  93.1 1.2 copy-start.8
  93.1 1.2 copy-start.15
  94.3 2.5 copy-start.10
  94.3 2.5 copy-start.12
  94.3 2.5 copy-start.20
  94.4 2.5 copy-start.23
  132.8 11.6 %copy-start.11 = (bf16[256,12,64]{0,2,1:T(8,128)(2,1)S(1)}, bf16[256,12,64]{0,2,1:T(8,128)(2,1)}, u32[]{:S(2)}) copy-start(bf16[256,12,64]{0,2,1:T(8,128)(2,1)} %get-tuple-element.17) | copy-start | bytes 1179652
  132.8 11.7 %copy-start.13 = (bf16[256,12,64]{0,2,1:T(8,128)(2,1)S(1)}, bf16[256,12,64]{0,2,1:T(8,128)(2,1)}, u32[]{:S(2)}) copy-start(bf16[256,12,64]{0,2,1:T(8,128)(2,1)} %get-tuple-element.15) | copy-start | bytes 1179652
  132.8 11.7 %copy-start.21 = (f32[256]{0:T(256)S(1)}, f32[256]{0:T(256)}, u32[]{:S(2)}) copy-start(f32[256]{0:T(256)} %copy-done.19) | copy-start | bytes 3076
  132.8 165.4 %all-to-all-start.1 = ((bf16[64,6,3072]{2,1,0:T(8,128)(2,1)}), bf16[64,6,3072]{2,1,0:T(8,128)(2,1)}, u32[]{:S(2)}, u32[]{:S(2)}) async-start(bf16[64,6,3072]{2,1,0:T(8,128)(2,1)} %copy.64), calls=%async_computation.1 | async-start | bytes 6291456 | tf_op jit(solution)/shard_map/all_to_all | solution.py:40
  144.5 3.3 %copy-start.7 = (bf16[256,12,64]{0,2,1:T(8,128)(2,1)S(1)}, bf16[256,12,64]{0,2,1:T(8,128)(2,1)}, u32[]{:S(2)}) copy-start(bf16[256,12,64]{0,2,1:T(8,128)(2,1)} %get-tuple-element.18) | copy-start | bytes 1179652
  144.5 3.3 %copy-start.9 = (bf16[256,12,64]{0,2,1:T(8,128)(2,1)S(1)}, bf16[256,12,64]{0,2,1:T(8,128)(2,1)}, u32[]{:S(2)}) copy-start(bf16[256,12,64]{0,2,1:T(8,128)(2,1)} %get-tuple-element.16) | copy-start | bytes 1179652
  144.5 3.3 %copy-start.16 = (bf16[12,64,256]{2,1,0:T(8,128)(2,1)S(1)}, bf16[12,64,256]{2,1,0:T(8,128)(2,1)}, u32[]{:S(2)}) copy-start(bf16[12,64,256]{2,1,0:T(8,128)(2,1)} %fusion.41) | copy-start | bytes 1179652
  144.5 3.3 %copy-start.24 = (bf16[768,2304]{1,0:T(8,128)(2,1)S(1)}, bf16[768,2304]{1,0:T(8,128)(2,1)}, u32[]{:S(2)}) copy-start(bf16[768,2304]{1,0:T(8,128)(2,1)} %param.10) | copy-start | bytes 10616836
  147.8 149.3 %copy-start.3 = (bf16[1,256,768]{2,1,0:T(8,128)(2,1)S(1)}, bf16[1,256,768]{2,1,0:T(8,128)(2,1)}, u32[]{:S(2)}) copy-start(bf16[1,256,768]{2,1,0:T(8,128)(2,1)} %param.7) | copy-start | bytes 1179652
  149.8 155.9 %copy-start.5 = (bf16[12,64,256]{2,1,0:T(8,128)(2,1)S(1)}, bf16[12,64,256]{2,1,0:T(8,128)(2,1)}, u32[]{:S(2)}) copy-start(bf16[12,64,256]{2,1,0:T(8,128)(2,1)} %copy-done.4) | copy-start | bytes 1179652
  301.4 10.1 %all-to-all-start.2 = ((bf16[2,6,3072]{2,1,0:T(8,128)(2,1)}), bf16[2,6,3072]{2,1,0:T(8,128)(2,1)S(1)}, u32[]{:S(2)}, u32[]{:S(2)}) async-start(bf16[2,6,3072]{2,1,0:T(8,128)(2,1)} %broadcast_in_dim.27), calls=%async_computation.2 | async-start | bytes 196608 | tf_op jit(solution)/shard_map/all_to_all | solution.py:46
